TPU v7x, 512 devices: a whole 4x8x8 slice. The times are simulated.
512 devices in a mesh: dp: 8 (over z), section: 4 (over x), patch: 16 (over y, core).
Axes of the slice: x: 4, y: 8, z: 8, core: 2. Of those that a mesh axis runs over, the one named last changes fastest.
Arguments:
- maps: bfloat16 [4, 8, 1536, 256], P(None, 'dp', 'patch'), may hold values from -6 to 6
- upstream: bfloat16 [4, 8, 1536, 256], P(None, 'dp', 'patch'), may hold values from -6 to 6
- weights: bfloat16 [4, 2304, 256], P('section'), may hold values from -0.125 to 0.125
- neighbours: int32 [9, 1536], P(None, 'patch'), may hold values from 0 to 1535, as said below
Outputs:
- input_grads: bfloat16 [4, 4, 8, 1536, 256], P('section', None, 'dp', 'patch')
- weight_grads: bfloat16 [4, 2304, 256], P('section')
Inputs may be any that keep to these rules, and one draw needn't show every extreme that they name: neighbours[0, p] = p; every entry is (p + d) mod 1536 with -32 <= d <= 32, and both d = 32 and d = -32 occur in every draw.
All inputs are finite; a program needn't handle non-finite values.
Results may differ from a plain program's by a relative error of at most 0.0063.
Values may be sent and summed in bfloat16 or wider, within the bound.
No kernel may reach another device: no remote copies, remote signals or barrier semaphores. Data moves between devices by JAX's collectives and lax.ppermute only.
A program may use at most 64 MiB of HBM per device.

v0:
```python
import jax
import jax.numpy as jnp
from jax import lax
from jax.sharding import PartitionSpec as P

HALO = 32


def extended_2(block, sides, width):
    for axis, dim in sides:
        count = lax.axis_size(axis)
        forward = [(i, i + 1) for i in range(count - 1)]
        forward.append((count - 1, 0))
        backward = [(target, source) for source, target in forward]
        low = lax.ppermute(
            lax.slice_in_dim(block, block.shape[dim] - width, None, axis=dim), axis, forward
        )
        high = lax.ppermute(lax.slice_in_dim(block, 0, width, axis=dim), axis, backward)
        block = jnp.concatenate([low, block, high], axis=dim)
    return block


def from_behind(shard, axis, by):
    size = lax.axis_size(axis)
    pairs = [(i, i + by) for i in range(size) if 0 <= i + by < size]
    return lax.ppermute(shard, axis, pairs)


def body(maps, upstream, weights, neighbours):
    micro = maps.shape[0]
    pix = maps.shape[2]
    chans = maps.shape[3]
    taps = neighbours.shape[0]
    sections = lax.axis_size("section")
    patches = lax.axis_size("patch")
    section_id = lax.axis_index("section")
    patch_id = lax.axis_index("patch")
    total = pix * patches
    local = jnp.mod(neighbours - patch_id * pix + HALO, total)
    index_rows = local.T.reshape(-1)
    w_flat = weights[0]
    w_taps = w_flat.reshape((taps, chans, chans))
    width = pix + 2 * HALO
    saved_ext = jnp.zeros((micro, width, chans), jnp.bfloat16)
    saved_tanh = jnp.zeros((micro, pix, chans), jnp.float32)
    incoming = jnp.zeros((pix, chans), jnp.bfloat16)
    for tick in range(micro + sections - 1):
        slot = tick - section_id
        valid = (slot >= 0) & (slot < micro)
        clipped = jnp.clip(slot, 0, micro - 1)
        current = jnp.where(section_id == 0, maps[min(tick, micro - 1), 0], incoming)
        extended = extended_2(current, (("patch", 0),), HALO)
        gathered = extended[index_rows].reshape((pix, taps * chans))
        act = jnp.dot(gathered, w_flat, preferred_element_type=jnp.float32)
        squash = jnp.tanh(act)
        result = (current.astype(jnp.float32) + squash).astype(jnp.bfloat16)
        saved_ext = saved_ext.at[clipped].set(jnp.where(valid, extended, saved_ext[clipped]))
        saved_tanh = saved_tanh.at[clipped].set(jnp.where(valid, squash, saved_tanh[clipped]))
        incoming = from_behind(result, "section", 1)
    grad_in = jnp.zeros((pix, chans), jnp.bfloat16)
    weight_acc = jnp.zeros((taps * chans, chans), jnp.float32)
    grads_out = jnp.zeros((micro, 1, pix, chans), jnp.bfloat16)
    for tick in range(micro + sections - 1):
        slot = tick - (sections - 1 - section_id)
        valid = (slot >= 0) & (slot < micro)
        clipped = jnp.clip(slot, 0, micro - 1)
        grad = jnp.where(section_id == sections - 1, upstream[min(tick, micro - 1), 0], grad_in)
        squash = saved_tanh[clipped]
        pre = (grad.astype(jnp.float32) * (1.0 - squash * squash)).astype(jnp.bfloat16)
        gathered = saved_ext[clipped][index_rows].reshape((pix, taps * chans))
        term = lax.dot_general(
            gathered, pre, (((0,), (0,)), ((), ())), preferred_element_type=jnp.float32
        )
        weight_acc = weight_acc + jnp.where(valid, term, 0.0)
        parts = jnp.einsum("qo,kio->qki", pre, w_taps, preferred_element_type=jnp.float32)
        spread = (
            jnp.zeros((width, chans), jnp.float32)
            .at[index_rows]
            .add(parts.reshape((pix * taps, chans)))
        )
        rims = jnp.concatenate([spread[:HALO], spread[pix + HALO :]], 0)
        returned = extended_2(rims, (("patch", 0),), HALO)
        own = spread[HALO : HALO + pix]
        own = own.at[:HALO].add(returned[:HALO])
        own = own.at[pix - HALO :].add(returned[3 * HALO :])
        dx_level = (grad.astype(jnp.float32) + own).astype(jnp.bfloat16)
        grads_out = grads_out.at[clipped, 0].set(jnp.where(valid, dx_level, grads_out[clipped, 0]))
        grad_in = from_behind(dx_level, "section", -1)
    summed = lax.psum(weight_acc, ("dp", "patch")).astype(jnp.bfloat16)
    return (grads_out[None], summed[None])


def solution(mesh):
    in_specs = (
        P(None, "dp", "patch", None),
        P(None, "dp", "patch", None),
        P("section", None, None),
        P(None, "patch"),
    )
    out_specs = (P("section", None, "dp", "patch", None), P("section", None, None))
    return jax.shard_map(body, mesh=mesh, in_specs=in_specs, out_specs=out_specs, check_vma=False)
```

profile of v0, /device:TPU:4, one launch (start us, length us, event | category | flops | bytes accessed | tf_op | source)
XLA Modules:
  0.0 830.5 jit_solution(4863639710440151621)
XLA Ops:
  1.6 2.9 collective-permute-start.1
  16.0 3.5 gather_fusion
  21.1 3.1 collective-permute-start.2
  24.2 2.8 collective-permute-done.2
  27.1 2.9 collective-permute-start.4
  31.5 3.5 gather_fusion.1
  36.5 3.1 collective-permute-start.5
  39.6 4.6 collective-permute-done.5
  44.3 2.9 collective-permute-start.7
  48.7 3.5 gather_fusion.2
  53.6 1.9 collective-permute-start.8
  55.6 4.0 collective-permute-done.8
  59.7 2.9 collective-permute-start.10
  64.1 3.5 gather_fusion.3
  71.0 4.0 collective-permute-done.11
  75.0 2.9 collective-permute-start.13
  79.4 3.5 gather_fusion.4
  86.4 4.0 collective-permute-done.14
  90.5 2.9 collective-permute-start.16
  94.8 3.5 gather_fusion.5
  99.8 2.1 collective-permute-start.17
  101.9 3.9 collective-permute-done.17
  105.8 2.9 collective-permute-start.19
  110.2 3.5 gather_fusion.6
  118.2 6.1 scatter_custom_fusion
  124.3 2.9 collective-permute-start.21
  130.4 3.9 collective-permute-start.22
  134.4 3.5 gather_fusion.7
  141.4 2.5 reshape.1373
  143.9 6.1 scatter_custom_fusion.1
  150.0 2.9 collective-permute-start.24
  155.3 2.1 collective-permute-start.25
  157.5 1.9 convolution_select_fusion.6
  159.4 3.5 gather_fusion.9
  164.1 3.5 gather_fusion.8
  168.9 3.5 gather_fusion.11
  173.6 3.5 gather_fusion.10
  178.3 3.5 gather_fusion.13
  183.1 3.5 gather_fusion.12
  189.9 6.1 scatter_custom_fusion.2
  196.9 3.0 collective-permute-start.27
  202.7 2.3 collective-permute-start.28
  205.0 2.9 convolution_select_fusion.4
  211.0 2.6 reshape.1389
  213.6 6.6 scatter_custom_fusion.3
  222.7 2.9 collective-permute-start.30
  227.3 2.2 fusion.110
  229.4 1.9 collective-permute-start.31
  231.4 3.8 fusion.5
  239.1 6.1 scatter_custom_fusion.4
  246.1 2.9 collective-permute-start.33
  250.6 2.0 fusion.107
  252.6 2.1 collective-permute-start.34
  256.2 2.3 collective-permute-done.34
  263.0 2.4 reshape.1405
  265.4 6.6 scatter_custom_fusion.5
  274.5 2.9 collective-permute-start.36
  279.1 2.2 fusion.104
  281.2 2.1 collective-permute-start.37
  283.3 2.3 fusion.4
  292.0 2.4 reshape.1413
  294.4 6.6 scatter_custom_fusion.6
  302.5 522.8 %all-reduce.1 = bf16[2304,256]{1,0:T(8,128)(2,1)} all-reduce(f32[2304,256]{1,0:T(8,128)S(1)} %fusion.3), channel_id=1, replica_groups=mesh['dp'=8,'section'=4,'patch'=16] {'dp','patch'}, use_global_device_ids=true, to_apply=%region_21.22 | all-reduce | flops 589824 | bytes 3538944 | tf_op jit(solution)/shard_map/psum | solution.py:89
  828.1 2.1 fusion.99
  (233 shorter events, 94.9 us)
Async XLA Ops:
  0.6 19.4 %copy-start = (bf16[1,2304,256]{2,1,0:T(8,128)(2,1)S(1)}, bf16[1,2304,256]{2,1,0:T(8,128)(2,1)}, u32[]{:S(2)}) copy-start(bf16[1,2304,256]{2,1,0:T(8,128)(2,1)} %param.76) | copy-start | bytes 3538948
  1.6 14.4 %collective-permute-start = (bf16[32,256]{1,0:T(8,128)(2,1)S(1)}, bf16[32,256]{1,0:T(8,128)(2,1)S(1)}, u32[]{:S(2)}, u32[]{:S(2)}) collective-permute-start(bf16[32,256]{1,0:T(8,128)(2,1)S(1)} %get-tuple-element.483), channel_id=1, source_target_pairs={{0,1},{1,2},{2,3},{3,4},{4,5},{5,6},{6,7},{7,8},{8,9},{9,10},{10,1... | collective-permute-start | bytes 49160 | tf_op jit(solution)/shard_map/ppermute | solution.py:15
  1.6 14.4 %collective-permute-start.1 = (bf16[32,256]{1,0:T(8,128)(2,1)S(1)}, bf16[32,256]{1,0:T(8,128)(2,1)S(1)}, u32[]{:S(2)}, u32[]{:S(2)}) collective-permute-start(bf16[32,256]{1,0:T(8,128)(2,1)S(1)} %get-tuple-element.484), channel_id=1, source_target_pairs={{1,0},{2,1},{3,2},{4,3},{5,4},{6,5},{7,6},{8,7},{9,8},{10,9},{11,1... | collective-permute-start | bytes 49160 | tf_op jit(solution)/shard_map/ppermute | solution.py:18
  19.5 1.6 copy-start.9
  21.1 6.0 collective-permute-start.2
  27.1 4.4 collective-permute-start.3
  27.1 4.4 collective-permute-start.4
  36.5 7.7 collective-permute-start.5
  44.3 4.4 collective-permute-start.6
  44.3 4.4 collective-permute-start.7
  53.6 6.0 collective-permute-start.8
  59.6 4.4 collective-permute-start.9
  59.7 4.4 collective-permute-start.10
  69.0 6.0 collective-permute-start.11
  75.0 4.4 collective-permute-start.12
  75.0 4.4 collective-permute-start.13
  84.4 6.0 collective-permute-start.14
  90.4 4.4 collective-permute-start.15
  90.5 4.4 collective-permute-start.16
  99.8 6.0 collective-permute-start.17
  105.8 4.4 collective-permute-start.18
  105.8 4.4 collective-permute-start.19
  110.2 3.5 copy-start.20
  115.2 93.5 %copy-start.2 = (f32[4,96,256]{2,1,0:T(8,128)}, f32[4,96,256]{2,1,0:T(8,128)S(1)}, u32[]{:S(2)}) copy-start(f32[4,96,256]{2,1,0:T(8,128)S(1)} %fusion.50) | copy-start | bytes 1179652
  124.3 4.6 collective-permute-start.20
  124.3 4.5 collective-permute-start.21
  130.4 8.8 %collective-permute-start.22 = (bf16[96,256]{1,0:T(8,128)(2,1)S(1)}, bf16[96,256]{1,0:T(8,128)(2,1)S(1)}, u32[]{:S(2)}, u32[]{:S(2)}) collective-permute-start(bf16[96,256]{1,0:T(8,128)(2,1)S(1)} %get-tuple-element.449), channel_id=1, source_target_pairs={{16,0},{32,16},{48,32},{17,1},{33,17},{49,33},{18,2},{34,18},{50,3... | collective-permute-start | bytes 147464 | tf_op jit(solution)/shard_map/ppermute | solution.py:26
  134.4 4.8 copy-start.3
  139.2 2.2 copy-start.10
  141.4 16.0 %copy-start.7 = (bf16[96,2304]{1,0:T(8,128)(2,1)S(1)}, bf16[96,2304]{1,0:T(8,128)(2,1)}, u32[]{:S(2)}) copy-start(bf16[96,2304]{1,0:T(8,128)(2,1)} %reshape.1241) | copy-start | bytes 1327108
  150.0 4.6 collective-permute-start.23
  150.0 4.5 collective-permute-start.24
  155.3 12.3 %copy-start.4 = (bf16[4,1,96,256]{3,2,1,0:T(8,128)(2,1)}, bf16[4,1,96,256]{3,2,1,0:T(8,128)(2,1)S(1)}, u32[]{:S(2)}) copy-start(bf16[4,1,96,256]{3,2,1,0:T(8,128)(2,1)S(1)} %get-tuple-element.446) | copy-start | bytes 589828
  155.3 32.5 %collective-permute-start.25 = (bf16[96,256]{1,0:T(8,128)(2,1)S(1)}, bf16[96,256]{1,0:T(8,128)(2,1)S(1)}, u32[]{:S(2)}, u32[]{:S(2)}) collective-permute-start(bf16[96,256]{1,0:T(8,128)(2,1)S(1)} %get-tuple-element.447), channel_id=1, source_target_pairs={{16,0},{32,16},{48,32},{17,1},{33,17},{49,33},{18,2},{34,18},{50,3... | collective-permute-start | bytes 147464 | tf_op jit(solution)/shard_map/ppermute | solution.py:26
  196.0 4.6 collective-permute-start.26
  196.9 4.5 collective-permute-start.27
  202.7 6.0 collective-permute-start.28
  208.7 0.6 copy-start.18
  208.7 0.6 copy-start.11
  211.0 20.4 %copy-start.1 = (f32[2304,256]{1,0:T(8,128)S(1)}, f32[2304,256]{1,0:T(8,128)}, u32[]{:S(2)}) copy-start(f32[2304,256]{1,0:T(8,128)} %convolution_select_fusion.6) | copy-start | bytes 7077892
  221.0 4.7 collective-permute-start.29
  222.7 4.5 collective-permute-start.30
  229.4 6.0 collective-permute-start.31
  235.4 2.1 copy-start.16
  236.4 0.6 copy-start.14
  238.1 12.6 %copy-start.17 = (bf16[96,256]{1,0:T(8,128)(2,1)S(1)}, bf16[96,256]{1,0:T(8,128)(2,1)}, u32[]{:S(2)}) copy-start(bf16[96,256]{1,0:T(8,128)(2,1)} %copy-done.16) | copy-start | bytes 147460
  245.2 4.6 collective-permute-start.32
  246.1 4.5 collective-permute-start.33
  252.6 6.0 collective-permute-start.34
  258.6 0.6 copy-start.19
  260.1 0.6 copy-start.12
  272.8 4.7 collective-permute-start.35
  274.5 4.5 collective-permute-start.36
  281.2 4.4 copy-start.5
  281.2 6.1 collective-permute-start.37
  285.6 3.1 copy-start.6
  287.3 0.9 copy-start.15
  288.8 1.0 copy-start.8
  288.8 1.0 copy-start.13
  302.5 523.8 %collective-permute-start.38 = (f32[32,256]{1,0:T(8,128)}, f32[32,256]{1,0:T(8,128)}, u32[]{:S(2)}, u32[]{:S(2)}) collective-permute-start(f32[32,256]{1,0:T(8,128)} %get-tuple-element.458), channel_id=1, source_target_pairs={{0,1},{1,2},{2,3},{3,4},{4,5},{5,6},{6,7},{7,8},{8,9},{9,10},{10,1... | collective-permute-start | bytes 98312 | tf_op jit(solution)/shard_map/ppermute | solution.py:15
  826.2 1.9 collective-permute-start.39
where the time goes:
time: 841 us; the launch traced here: 830 us
  blocking collectives  523 us (62%)
  local copies, waits for them, and re-layouts  94.9 us (11%)
  other arithmetic  79 us (9%)
  starting transfers between devices  67.1 us (8%)
  waiting for transfers between devices  39.9 us (5%)
  matrix products  24.8 us (3%)
    psum x1, blocking collectives, body(): summed = lax.psum(weight_acc, ('dp', 'patch')).astype(jnp.bfloat16)  523 us
    scatter-add x7, other arithmetic, body(): spread = jnp.zeros((width, chans), jnp.float32).at[index_rows].add(parts....  44.2 us
    ppermute x14, starting transfers between devices, extended_2(): lax.ppermute(lax.slice_in_dim(block, 0, width, axis=dim), axis, backward)  38.3 us
    ppermute x12, starting transfers between devices, from_behind(): return lax.ppermute(shard, axis, pairs)  28.6 us
    ppermute x12, waiting for transfers between devices, from_behind(): return lax.ppermute(shard, axis, pairs)  27.6 us
    gather x7, local copies, waits for them, and re-layouts, body(): gathered = extended[index_rows].reshape((pix, taps * chans))  24.2 us
    gather x7, local copies, waits for them, and re-layouts, body(): gathered = saved_ext[clipped][index_rows].reshape((pix, taps * chans))  24.2 us
  transfers between devices with their start and end apart: 40, of which 25 were waited for; matrix products, arithmetic and copies ran while one was open for 9% of the time, Pallas kernels for 0%

commit v1 on v0

--- a/solution.py
+++ b/solution.py
@@ -27,6 +27,14 @@
 
 
 def body(maps, upstream, weights, neighbours):
+
+    def lane_use(page):
+        axis_tag = "dp"
+        mesh_ax = "patch"
+        for k in (mesh_ax, axis_tag):
+            page = jax.lax.psum(page, axis_name=k)
+        return page
+
     micro = maps.shape[0]
     pix = maps.shape[2]
     chans = maps.shape[3]
@@ -86,7 +94,7 @@
         dx_level = (grad.astype(jnp.float32) + own).astype(jnp.bfloat16)
         grads_out = grads_out.at[clipped, 0].set(jnp.where(valid, dx_level, grads_out[clipped, 0]))
         grad_in = from_behind(dx_level, "section", -1)
-    summed = lax.psum(weight_acc, ("dp", "patch")).astype(jnp.bfloat16)
+    summed = lane_use(weight_acc).astype(jnp.bfloat16)
     return (grads_out[None], summed[None])
 
 

time: 841 us -> 507 us (0.60)
  the two profiles are of different devices: /device:TPU:4 before, /device:TPU:32 now
where the time goes in v1:
time: 507 us; the launch traced here: 497 us
  waiting for transfers between devices  144 us (28%)
  local copies, waits for them, and re-layouts  89.6 us (18%)
  other arithmetic  76.5 us (15%)
  starting transfers between devices  74.9 us (15%)
  blocking collectives  70.1 us (14%)
  matrix products  26.1 us (5%)
  between operations  15.5 us (3%)
    psum x1, waiting for transfers between devices, lane_use(): page = jax.lax.psum(page, axis_name=k)  112 us
    psum x1, blocking collectives, lane_use(): page = jax.lax.psum(page, axis_name=k)  70.1 us
    scatter-add x7, other arithmetic, body(): spread = jnp.zeros((width, chans), jnp.float32).at[index_rows].add(parts....  43.6 us
    ppermute x14, starting transfers between devices, extended_2(): lax.ppermute(lax.slice_in_dim(block, 0, width, axis=dim), axis, backward)  41.2 us
    ppermute x12, starting transfers between devices, from_behind(): return lax.ppermute(shard, axis, pairs)  33.4 us
    gather x7, local copies, waits for them, and re-layouts, body(): gathered = extended[index_rows].reshape((pix, taps * chans))  24.2 us
    gather x7, local copies, waits for them, and re-layouts, body(): gathered = saved_ext[clipped][index_rows].reshape((pix, taps * chans))  24.2 us
    ppermute x12, waiting for transfers between devices, from_behind(): return lax.ppermute(shard, axis, pairs)  19.2 us
  transfers between devices with their start and end apart: 41, of which 27 were waited for; matrix products, arithmetic and copies ran while one was open for 16% of the time, Pallas kernels for 0%

profile of v1, /device:TPU:32, one launch (start us, length us, event | category | flops | bytes accessed | tf_op | source)
XLA Modules:
  0.0 496.8 jit_solution(16115502438284134906)
XLA Ops:
  8.2 2.9 collective-permute-start.1
  22.5 3.5 gather_fusion
  27.6 3.4 collective-permute-start.2
  31.0 1.7 collective-permute-done.2
  32.7 2.9 collective-permute-start.4
  37.1 3.5 gather_fusion.1
  42.1 4.2 collective-permute-start.5
  46.4 1.7 collective-permute-done.5
  48.1 2.9 collective-permute-start.7
  52.5 3.5 gather_fusion.2
  57.4 4.2 collective-permute-start.8
  61.7 1.7 collective-permute-done.8
  63.4 2.9 collective-permute-start.10
  67.8 3.5 gather_fusion.3
  72.8 4.2 collective-permute-start.11
  78.8 2.9 collective-permute-start.13
  83.2 3.5 gather_fusion.4
  88.2 4.2 collective-permute-start.14
  92.5 1.7 collective-permute-done.14
  94.2 2.9 collective-permute-start.16
  98.6 3.5 gather_fusion.5
  103.6 4.4 collective-permute-start.17
  109.6 2.9 collective-permute-start.19
  114.0 3.5 gather_fusion.6
  121.9 6.1 %scatter_custom_fusion = f32[160,256]{1,0:T(8,128)S(1)} fusion(s32[864]{0:T(1024)S(1)} %fusion.135, f32[864,256]{1,0:T(8,128)} %reshape.1365, f32[]{:T(128)} %constant.778.clone.1), kind=kCustom, calls=%fused_computation.152 | custom fusion | flops 221184 | bytes 164352 | tf_op jit(solution)/shard_map/scatter-add | solution.py:87
  128.0 2.9 collective-permute-start.21
  135.4 3.5 gather_fusion.7
  140.9 1.7 copy.17
  142.6 2.5 reshape.1373
  145.1 6.1 %scatter_custom_fusion.1 = f32[160,256]{1,0:T(8,128)S(1)} fusion(s32[864]{0:T(1024)S(1)} %fusion.135, f32[864,256]{1,0:T(8,128)} %reshape.1373, f32[]{:T(128)} %constant.778.clone.1), kind=kCustom, calls=%fused_computation.150 | custom fusion | flops 221184 | bytes 164352 | tf_op jit(solution)/shard_map/scatter-add | solution.py:87
  151.2 2.9 collective-permute-start.24
  158.0 1.9 convolution_select_fusion.6
  159.9 3.5 gather_fusion.9
  164.6 3.5 gather_fusion.8
  169.4 3.5 gather_fusion.11
  174.1 3.5 gather_fusion.10
  178.9 3.5 gather_fusion.13
  183.6 3.5 gather_fusion.12
  190.4 6.1 %scatter_custom_fusion.2 = f32[160,256]{1,0:T(8,128)S(1)} fusion(s32[864]{0:T(1024)S(1)} %fusion.135, f32[864,256]{1,0:T(8,128)} %reshape.1381, f32[]{:T(128)} %constant.778.clone.1), kind=kCustom, calls=%fused_computation.148 | custom fusion | flops 221184 | bytes 164352 | tf_op jit(solution)/shard_map/scatter-add | solution.py:87
  197.4 3.0 collective-permute-start.27
  204.9 3.0 convolution_select_fusion.4
  207.9 2.7 collective-permute-done.28
  211.2 1.8 copy.19
  213.0 2.6 reshape.1389
  215.6 6.7 %scatter_custom_fusion.3 = f32[160,256]{1,0:T(8,128)} fusion(s32[864]{0:T(1024)S(1)} %fusion.135, f32[864,256]{1,0:T(8,128)} %reshape.1389, f32[]{:T(128)} %constant.778.clone.1), kind=kCustom, calls=%fused_computation.146 | custom fusion | flops 221184 | bytes 164352 | tf_op jit(solution)/shard_map/scatter-add | solution.py:87
  224.7 2.9 collective-permute-start.30
  229.3 2.1 fusion.110
  232.7 3.8 fusion.5
  241.1 6.1 %scatter_custom_fusion.4 = f32[160,256]{1,0:T(8,128)S(1)} fusion(s32[864]{0:T(1024)S(1)} %fusion.135, f32[864,256]{1,0:T(8,128)} %reshape.1397, f32[]{:T(128)} %constant.778.clone.1), kind=kCustom, calls=%fused_computation.144 | custom fusion | flops 221184 | bytes 164352 | tf_op jit(solution)/shard_map/scatter-add | solution.py:87
  248.0 2.9 collective-permute-start.33
  252.5 2.1 fusion.107
  257.7 3.0 collective-permute-done.34
  263.3 1.7 copy.21
  265.1 2.4 reshape.1405
  267.5 6.6 %scatter_custom_fusion.5 = f32[160,256]{1,0:T(8,128)} fusion(s32[864]{0:T(1024)S(1)} %fusion.135, f32[864,256]{1,0:T(8,128)} %reshape.1405, f32[]{:T(128)} %constant.778.clone.1), kind=kCustom, calls=%fused_computation.142 | custom fusion | flops 221184 | bytes 164352 | tf_op jit(solution)/shard_map/scatter-add | solution.py:87
  276.6 2.9 collective-permute-start.36
  281.2 2.0 fusion.104
  284.6 2.3 fusion.4
  287.0 2.3 collective-permute-done.37
  291.4 1.9 fusion.3
  295.5 6.1 %scatter_custom_fusion.6 = f32[160,256]{1,0:T(8,128)S(1)} fusion(s32[864]{0:T(1024)S(1)} %fusion.135, f32[864,256]{1,0:T(8,128)} %reshape.1413, f32[]{:T(128)} %constant.778.clone.1), kind=kCustom, calls=%fused_computation.140 | custom fusion | flops 221184 | bytes 164352 | tf_op jit(solution)/shard_map/scatter-add | solution.py:87
  301.6 2.9 collective-permute-start.39
  307.7 112.0 %all-reduce.3.cloned.1.call-done = f32[2304,256]{1,0:T(8,128)} async-done(((f32[2304,256]{1,0:T(8,128)}), f32[2304,256]{1,0:T(8,128)}) %all-reduce.3.cloned.1.call-update) | async-done | bytes 2359312 | tf_op jit(solution)/shard_map/psum | solution.py:35
  419.7 70.1 %all-reduce.4 = bf16[2304,256]{1,0:T(8,128)(2,1)} all-reduce(f32[2304,256]{1,0:T(8,128)} %all-reduce.3.cloned.1.call-done), channel_id=1, replica_groups=mesh['dp'=8,'section'=4,'patch'=16] {'dp'}, use_global_device_ids=true, to_apply=%region_22.23 | all-reduce | flops 589824 | bytes 3538944 | tf_op jit(solution)/shard_map/psum | solution.py:35
  (240 shorter events, 94.3 us)
Async XLA Ops:
  7.2 19.3 %copy-start = (bf16[1,2304,256]{2,1,0:T(8,128)(2,1)S(1)}, bf16[1,2304,256]{2,1,0:T(8,128)(2,1)}, u32[]{:S(2)}) copy-start(bf16[1,2304,256]{2,1,0:T(8,128)(2,1)} %param.76) | copy-start | bytes 3538948
  7.2 412.5 %all-reduce.3.cloned.1.call-start = ((), (), s32[]{:S(2)}) async-start(), calls=%async_computation | async-start | bytes 4718592 | tf_op jit(solution)/shard_map/psum | solution.py:35
  8.1 14.3 %collective-permute-start = (bf16[32,256]{1,0:T(8,128)(2,1)S(1)}, bf16[32,256]{1,0:T(8,128)(2,1)S(1)}, u32[]{:S(2)}, u32[]{:S(2)}) collective-permute-start(bf16[32,256]{1,0:T(8,128)(2,1)S(1)} %get-tuple-element.483), channel_id=1, source_target_pairs={{0,1},{1,2},{2,3},{3,4},{4,5},{5,6},{6,7},{7,8},{8,9},{9,10},{10,1... | collective-permute-start | bytes 49160 | tf_op jit(solution)/shard_map/ppermute | solution.py:15
  8.2 14.3 %collective-permute-start.1 = (bf16[32,256]{1,0:T(8,128)(2,1)S(1)}, bf16[32,256]{1,0:T(8,128)(2,1)S(1)}, u32[]{:S(2)}, u32[]{:S(2)}) collective-permute-start(bf16[32,256]{1,0:T(8,128)(2,1)S(1)} %get-tuple-element.484), channel_id=1, source_target_pairs={{1,0},{2,1},{3,2},{4,3},{5,4},{6,5},{7,6},{8,7},{9,8},{10,9},{11,1... | collective-permute-start | bytes 49160 | tf_op jit(solution)/shard_map/ppermute | solution.py:18
  26.0 1.6 copy-start.9
  27.6 5.1 %collective-permute-start.2 = (bf16[96,256]{1,0:T(8,128)(2,1)S(1)}, bf16[96,256]{1,0:T(8,128)(2,1)S(1)}, u32[]{:S(2)}, u32[]{:S(2)}) collective-permute-start(bf16[96,256]{1,0:T(8,128)(2,1)S(1)} %add_convert_fusion.5), channel_id=1, source_target_pairs={{0,16},{16,32},{32,48},{1,17},{17,33},{33,49},{2,18},{18,34},{34,5... | collective-permute-start | bytes 147464 | tf_op jit(solution)/shard_map/ppermute | solution.py:26
  32.7 4.4 collective-permute-start.3
  32.7 4.4 collective-permute-start.4
  42.1 6.0 %collective-permute-start.5 = (bf16[96,256]{1,0:T(8,128)(2,1)S(1)}, bf16[96,256]{1,0:T(8,128)(2,1)S(1)}, u32[]{:S(2)}, u32[]{:S(2)}) collective-permute-start(bf16[96,256]{1,0:T(8,128)(2,1)S(1)} %add_convert_fusion.4), channel_id=1, source_target_pairs={{0,16},{16,32},{32,48},{1,17},{17,33},{33,49},{2,18},{18,34},{34,5... | collective-permute-start | bytes 147464 | tf_op jit(solution)/shard_map/ppermute | solution.py:26
  48.1 4.4 collective-permute-start.6
  48.1 4.4 collective-permute-start.7
  57.4 6.0 %collective-permute-start.8 = (bf16[96,256]{1,0:T(8,128)(2,1)S(1)}, bf16[96,256]{1,0:T(8,128)(2,1)S(1)}, u32[]{:S(2)}, u32[]{:S(2)}) collective-permute-start(bf16[96,256]{1,0:T(8,128)(2,1)S(1)} %add_convert_fusion.3), channel_id=1, source_target_pairs={{0,16},{16,32},{32,48},{1,17},{17,33},{33,49},{2,18},{18,34},{34,5... | collective-permute-start | bytes 147464 | tf_op jit(solution)/shard_map/ppermute | solution.py:26
  63.4 4.4 collective-permute-start.9
  63.4 4.4 collective-permute-start.10
  72.8 6.0 %collective-permute-start.11 = (bf16[96,256]{1,0:T(8,128)(2,1)S(1)}, bf16[96,256]{1,0:T(8,128)(2,1)S(1)}, u32[]{:S(2)}, u32[]{:S(2)}) collective-permute-start(bf16[96,256]{1,0:T(8,128)(2,1)S(1)} %add_convert_fusion.2), channel_id=1, source_target_pairs={{0,16},{16,32},{32,48},{1,17},{17,33},{33,49},{2,18},{18,34},{34,5... | collective-permute-start | bytes 147464 | tf_op jit(solution)/shard_map/ppermute | solution.py:26
  78.8 4.4 collective-permute-start.12
  78.8 4.4 collective-permute-start.13
  88.2 6.0 %collective-permute-start.14 = (bf16[96,256]{1,0:T(8,128)(2,1)S(1)}, bf16[96,256]{1,0:T(8,128)(2,1)S(1)}, u32[]{:S(2)}, u32[]{:S(2)}) collective-permute-start(bf16[96,256]{1,0:T(8,128)(2,1)S(1)} %add_convert_fusion.1), channel_id=1, source_target_pairs={{0,16},{16,32},{32,48},{1,17},{17,33},{33,49},{2,18},{18,34},{34,5... | collective-permute-start | bytes 147464 | tf_op jit(solution)/shard_map/ppermute | solution.py:26
  94.2 4.4 collective-permute-start.15
  94.2 4.4 collective-permute-start.16
  103.6 6.0 %collective-permute-start.17 = (bf16[96,256]{1,0:T(8,128)(2,1)S(1)}, bf16[96,256]{1,0:T(8,128)(2,1)S(1)}, u32[]{:S(2)}, u32[]{:S(2)}) collective-permute-start(bf16[96,256]{1,0:T(8,128)(2,1)S(1)} %add_convert_fusion), channel_id=1, source_target_pairs={{0,16},{16,32},{32,48},{1,17},{17,33},{33,49},{2,18},{18,34},{34,5... | collective-permute-start | bytes 147464 | tf_op jit(solution)/shard_map/ppermute | solution.py:26
  109.6 4.4 collective-permute-start.18
  109.6 4.4 collective-permute-start.19
  114.0 3.5 copy-start.22
  118.9 91.7 %copy-start.2 = (f32[4,96,256]{2,1,0:T(8,128)}, f32[4,96,256]{2,1,0:T(8,128)S(1)}, u32[]{:S(2)}) copy-start(f32[4,96,256]{2,1,0:T(8,128)S(1)} %fusion.50) | copy-start | bytes 1179652
  128.0 4.6 collective-permute-start.20
  128.0 4.5 collective-permute-start.21
  134.0 6.3 %collective-permute-start.22 = (bf16[96,256]{1,0:T(8,128)(2,1)S(1)}, bf16[96,256]{1,0:T(8,128)(2,1)S(1)}, u32[]{:S(2)}, u32[]{:S(2)}) collective-permute-start(bf16[96,256]{1,0:T(8,128)(2,1)S(1)} %get-tuple-element.449), channel_id=1, source_target_pairs={{16,0},{32,16},{48,32},{17,1},{33,17},{49,33},{18,2},{34,18},{50,3... | collective-permute-start | bytes 147464 | tf_op jit(solution)/shard_map/ppermute | solution.py:26
  135.4 4.9 copy-start.3
  140.4 2.3 copy-start.10
  142.6 15.3 %copy-start.7 = (bf16[96,2304]{1,0:T(8,128)(2,1)S(1)}, bf16[96,2304]{1,0:T(8,128)(2,1)}, u32[]{:S(2)}) copy-start(bf16[96,2304]{1,0:T(8,128)(2,1)} %reshape.1241) | copy-start | bytes 1327108
  151.2 4.6 collective-permute-start.23
  151.2 4.5 collective-permute-start.24
  156.4 11.7 %copy-start.4 = (bf16[4,1,96,256]{3,2,1,0:T(8,128)(2,1)}, bf16[4,1,96,256]{3,2,1,0:T(8,128)(2,1)S(1)}, u32[]{:S(2)}) copy-start(bf16[4,1,96,256]{3,2,1,0:T(8,128)(2,1)S(1)} %get-tuple-element.446) | copy-start | bytes 589828
  156.4 31.8 %collective-permute-start.25 = (bf16[96,256]{1,0:T(8,128)(2,1)S(1)}, bf16[96,256]{1,0:T(8,128)(2,1)S(1)}, u32[]{:S(2)}, u32[]{:S(2)}) collective-permute-start(bf16[96,256]{1,0:T(8,128)(2,1)S(1)} %get-tuple-element.447), channel_id=1, source_target_pairs={{16,0},{32,16},{48,32},{17,1},{33,17},{49,33},{18,2},{34,18},{50,3... | collective-permute-start | bytes 147464 | tf_op jit(solution)/shard_map/ppermute | solution.py:26
  196.5 4.6 collective-permute-start.26
  197.4 4.6 collective-permute-start.27
  203.2 7.4 %collective-permute-start.28 = (bf16[96,256]{1,0:T(8,128)(2,1)S(1)}, bf16[96,256]{1,0:T(8,128)(2,1)S(1)}, u32[]{:S(2)}, u32[]{:S(2)}) collective-permute-start(bf16[96,256]{1,0:T(8,128)(2,1)S(1)} %get-tuple-element.445), channel_id=1, source_target_pairs={{16,0},{32,16},{48,32},{17,1},{33,17},{49,33},{18,2},{34,18},{50,3... | collective-permute-start | bytes 147464 | tf_op jit(solution)/shard_map/ppermute | solution.py:26
  210.6 0.6 copy-start.20
  210.6 0.6 copy-start.11
  213.0 19.7 %copy-start.1 = (f32[2304,256]{1,0:T(8,128)S(1)}, f32[2304,256]{1,0:T(8,128)}, u32[]{:S(2)}) copy-start(f32[2304,256]{1,0:T(8,128)} %convolution_select_fusion.6) | copy-start | bytes 7077892
  223.0 4.7 collective-permute-start.29
  224.7 4.5 collective-permute-start.30
  231.4 6.0 %collective-permute-start.31 = (bf16[96,256]{1,0:T(8,128)(2,1)S(1)}, bf16[96,256]{1,0:T(8,128)(2,1)S(1)}, u32[]{:S(2)}, u32[]{:S(2)}) collective-permute-start(bf16[96,256]{1,0:T(8,128)(2,1)S(1)} %get-tuple-element.443), channel_id=1, source_target_pairs={{16,0},{32,16},{48,32},{17,1},{33,17},{49,33},{18,2},{34,18},{50,3... | collective-permute-start | bytes 147464 | tf_op jit(solution)/shard_map/ppermute | solution.py:26
  237.3 2.1 copy-start.18
  238.3 0.6 copy-start.14
  240.0 12.6 %copy-start.19 = (bf16[96,256]{1,0:T(8,128)(2,1)S(1)}, bf16[96,256]{1,0:T(8,128)(2,1)}, u32[]{:S(2)}) copy-start(bf16[96,256]{1,0:T(8,128)(2,1)} %copy-done.18) | copy-start | bytes 147460
  247.1 4.6 collective-permute-start.32
  248.0 4.5 collective-permute-start.33
  254.7 6.0 %collective-permute-start.34 = (bf16[96,256]{1,0:T(8,128)(2,1)S(1)}, bf16[96,256]{1,0:T(8,128)(2,1)S(1)}, u32[]{:S(2)}, u32[]{:S(2)}) collective-permute-start(bf16[96,256]{1,0:T(8,128)(2,1)S(1)} %get-tuple-element.441), channel_id=1, source_target_pairs={{16,0},{32,16},{48,32},{17,1},{33,17},{49,33},{18,2},{34,18},{50,3... | collective-permute-start | bytes 147464 | tf_op jit(solution)/shard_map/ppermute | solution.py:26
  260.7 0.6 copy-start.21
  262.2 0.6 copy-start.12
  274.9 4.7 collective-permute-start.35
  276.6 4.5 collective-permute-start.36
  283.2 7.6 %copy-start.6 = (bf16[96,2304]{1,0:T(8,128)(2,1)S(1)}, bf16[96,2304]{1,0:T(8,128)(2,1)}, u32[]{:S(2)}) copy-start(bf16[96,2304]{1,0:T(8,128)(2,1)} %reshape.1247) | copy-start | bytes 1327108
  283.2 6.1 %collective-permute-start.37 = (bf16[96,256]{1,0:T(8,128)(2,1)S(1)}, bf16[96,256]{1,0:T(8,128)(2,1)S(1)}, u32[]{:S(2)}, u32[]{:S(2)}) collective-permute-start(bf16[96,256]{1,0:T(8,128)(2,1)S(1)} %get-tuple-element.439), channel_id=1, source_target_pairs={{16,0},{32,16},{48,32},{17,1},{33,17},{49,33},{18,2},{34,18},{50,3... | collective-permute-start | bytes 147464 | tf_op jit(solution)/shard_map/ppermute | solution.py:26
  287.0 4.4 copy-start.8
  287.0 4.4 copy-start.13
  289.3 0.6 copy-start.16
  294.4 7.2 %copy-start.5 = (bf16[4,1,96,256]{3,2,1,0:T(8,128)(2,1)S(1)}, bf16[4,1,96,256]{3,2,1,0:T(8,128)(2,1)}, u32[]{:S(2)}) copy-start(bf16[4,1,96,256]{3,2,1,0:T(8,128)(2,1)} %get-tuple-element.438) | copy-start | bytes 589828
  294.4 11.8 %copy-start.17 = (bf16[96,256]{1,0:T(8,128)(2,1)S(1)}, bf16[96,256]{1,0:T(8,128)(2,1)}, u32[]{:S(2)}) copy-start(bf16[96,256]{1,0:T(8,128)(2,1)} %copy-done.16) | copy-start | bytes 147460
  301.6 4.6 collective-permute-start.38
  301.6 4.5 collective-permute-start.39
  307.7 182.1 %copy-start.15 = (bf16[1,4,1,96,256]{4,3,1,2,0:T(8,128)(2,1)}, bf16[1,4,1,96,256]{4,3,1,2,0:T(8,128)(2,1)S(1)}, u32[]{:S(2)}) copy-start(bf16[1,4,1,96,256]{4,3,1,2,0:T(8,128)(2,1)S(1)} %fusion.99) | copy-start | bytes 589828
Sparse Core Ops, SparseCore 0:
  293.5 126.1 all-reduce.2
